TPU v7x, 32 devices: a whole 2x2x4 slice. The times are simulated.
32 devices in a mesh: rows: 16 (over z, y, x), feat: 2 (over core).
Axes of the slice: x: 2, y: 2, z: 4, core: 2. Of those that a mesh axis runs over, the one named last changes fastest.
Arguments:
- embeddings: bfloat16 [12288, 768], P('rows', 'feat'), may hold values from -6 to 6
- factor: float32 [12288, 256], P(('rows', 'feat')), may hold values from -0.1 to 0.1, as said below
- residual_diag: float32 [12288], P(('rows', 'feat')), may hold values from 0.5 to 1.5
- pivots: int32 [2, 256], replicated, may hold values from 0 to 12287, as said below
Outputs:
- new_columns: float32 [2, 12288, 256], P(None, ('rows', 'feat'))
- residual_out: float32 [12288], P(('rows', 'feat'))
Inputs may be any that keep to these rules, and one draw needn't show every extreme that they name: Each block's 256 pivots are distinct and increasing, the two blocks share none, and in each block at most 32 pivots lie among the 768 candidates of one index of rows; some index holds exactly 32 in every block. `factor`: entries are independent.
All inputs are finite; a program needn't handle non-finite values.
Results may differ from a plain program's by a relative error of at most 0.0003.
Values may be sent and summed in bfloat16 or wider, within the bound.
No kernel may reach another device: no remote copies, remote signals or barrier semaphores. Data moves between devices by JAX's collectives and lax.ppermute only.
A program may use at most 64 MiB of HBM per device.

v0:
```python
import jax
import jax.numpy as jnp
from jax import lax
from jax.sharding import PartitionSpec as P

ridge_weight = 2.0


def shards(embeddings, factor, residual_diag, pivots):
    local_rows = embeddings.shape[0]
    half_rows = factor.shape[0]
    feat_cols = embeddings.shape[1]
    feat_count = lax.axis_size("feat")
    full_width = feat_cols * feat_count
    row_group = lax.axis_index("rows")
    feat_group = lax.axis_index("feat")
    rows_start = row_group * local_rows
    half_start = rows_start + feat_group * half_rows
    global_ids = half_start + jnp.arange(half_rows, dtype=jnp.int32)
    partial_norms = jnp.sum(jnp.square(embeddings.astype(jnp.float32)), axis=1)
    row_norms = partial_norms
    current = factor
    fresh_list = []
    for block_id in range(2):
        chosen_ids = pivots[block_id]
        pivot_count = chosen_ids.shape[0]
        offsets = chosen_ids - rows_start
        owned_mask = (offsets >= 0) & (offsets < local_rows)
        safe_rows = jnp.clip(offsets, 0, local_rows - 1)
        half_offsets = offsets - feat_group * half_rows
        half_mask = owned_mask & (half_offsets >= 0) & (half_offsets < half_rows)
        half_safe = jnp.clip(half_offsets, 0, half_rows - 1)
        capacity = max(2, 2 * pivot_count // lax.axis_size("rows"))
        owners = chosen_ids // local_rows
        earlier = jnp.sum((owners[None, :] < owners[:, None]).astype(jnp.int32), axis=1)
        pivot_ranks = jnp.arange(pivot_count, dtype=jnp.int32) - earlier
        slot_hits = (
            pivot_ranks[None, :] == jnp.arange(capacity, dtype=jnp.int32)[:, None]
        ) & owned_mask[None, :]
        slot_full = jnp.any(slot_hits, axis=1)
        slot_rows = jnp.sum(jnp.where(slot_hits, safe_rows[None, :], 0), axis=1)
        half_hits = slot_hits & half_mask[None, :]
        slot_half = jnp.any(half_hits, axis=1)
        slot_half_rows = jnp.sum(jnp.where(half_hits, half_safe[None, :], 0), axis=1)
        packed_x = jnp.where(slot_full[:, None], jnp.take(embeddings, slot_rows, axis=0), 0)
        packed_f = jnp.where(slot_half[:, None], jnp.take(current, slot_half_rows, axis=0), 0.0)
        all_x = lax.all_gather(packed_x, ("rows", "feat"), axis=0, tiled=True)
        all_f = lax.all_gather(packed_f, ("rows", "feat"), axis=0, tiled=True)
        first_src = owners * feat_count * capacity + pivot_ranks
        pieces = []
        pivot_factor = jnp.zeros((pivot_count, current.shape[1]), jnp.float32)
        for feat_id in range(feat_count):
            source = first_src + feat_id * capacity
            pieces.append(jnp.take(all_x, source, axis=0))
            pivot_factor = pivot_factor + jnp.take(all_f, source, axis=0)
        chosen = jnp.concatenate(pieces, axis=1)
        own_cols = lax.dynamic_slice_in_dim(chosen, feat_group * feat_cols, feat_cols, 1)
        dots_part = jnp.einsum(
            "nd,kd->nk", embeddings, own_cols, preferred_element_type=jnp.float32
        )
        partial_terms = (dots_part, partial_norms) if block_id == 0 else (dots_part,)
        summed = lax.psum_scatter(partial_terms, "feat", scatter_dimension=0, tiled=True)
        dot_panel = summed[0]
        if block_id == 0:
            row_norms = summed[1]
        chosen_wide = chosen.astype(jnp.float32)
        chosen_norms = jnp.sum(chosen_wide * chosen_wide, axis=1)
        kernel_panel = jnp.exp(
            -(row_norms[:, None] + chosen_norms[None, :] - 2.0 * dot_panel) / (2.0 * full_width)
        )
        kernel_panel = kernel_panel + ridge_weight * (
            global_ids[:, None] == chosen_ids[None, :]
        ).astype(jnp.float32)
        kernel_panel = kernel_panel - jnp.dot(
            current,
            pivot_factor.T,
            precision=lax.Precision.HIGHEST,
            preferred_element_type=jnp.float32,
        )
        pivot_dots = jnp.einsum("kd,jd->kj", chosen, chosen, preferred_element_type=jnp.float32)
        pivot_block = jnp.exp(
            -(chosen_norms[:, None] + chosen_norms[None, :] - 2.0 * pivot_dots) / (2.0 * full_width)
        )
        pivot_block = pivot_block + ridge_weight * jnp.eye(pivot_count, dtype=jnp.float32)
        pivot_block = pivot_block - jnp.dot(
            pivot_factor,
            pivot_factor.T,
            precision=lax.Precision.HIGHEST,
            preferred_element_type=jnp.float32,
        )
        chol_lower = jnp.linalg.cholesky(pivot_block)
        fresh_cols = jax.scipy.linalg.solve_triangular(chol_lower, kernel_panel.T, lower=True).T
        fresh_list.append(fresh_cols)
        current = jnp.concatenate([current, fresh_cols], axis=1)
    removed = jnp.sum(fresh_list[0] * fresh_list[0], axis=1) + jnp.sum(
        fresh_list[1] * fresh_list[1], axis=1
    )
    return (jnp.stack(fresh_list), residual_diag - removed)


def solution(mesh):
    return jax.shard_map(
        shards,
        mesh=mesh,
        in_specs=(P("rows", "feat"), P(("rows", "feat"), None), P(("rows", "feat")), P()),
        out_specs=(P(None, ("rows", "feat"), None), P(("rows", "feat"))),
        check_vma=False,
    )
```

profile of v0, /device:TPU:0, one launch (start us, length us, event | category | flops | bytes accessed | tf_op | source)
XLA Modules:
  0.0 285.8 jit_solution(14113380142749730828)
XLA Ops:
  8.0 0.8 broadcast_clamp_fusion.1
  8.8 0.8 and_reduce_fusion
  10.1 1.6 gather_fusion
  11.7 0.7 select_select_fusion.3
  12.5 1.8 gather_fusion.2
  14.4 45.6 %all_gather.12 = bf16[1024,384]{1,0:T(8,128)(2,1)S(1)} all-gather(bf16[32,384]{1,0:T(8,128)(2,1)S(1)} %select_select_fusion.5), channel_id=1, replica_groups=mesh['rows'=16,'feat'=2] {'rows','feat'}, dimensions={0}, use_global_device_ids=true | all-gather | bytes 811008 | tf_op jit(solution)/shard_map/all_gather | solution.py:47
  60.1 1.2 gather_fusion.4
  61.2 1.2 gather_fusion.3
  62.6 1.3 convolution_bitcast_fusion.1
  66.5 0.7 fusion.43
  67.5 2.8 all-reduce.1
  72.3 2.3 gather_fusion.5
  74.5 1.0 gather_fusion.6
  76.3 11.7 %cholesky.130 = f32[128,128]{1,0:T(8,128)S(1)} custom-call(f32[128,128]{1,0:T(8,128)S(1)} %cholesky.194), custom_call_target="Cholesky" | custom-call | tf_op jit(solution)/shard_map/jit(cholesky)/cholesky | solution.py:91
  88.1 9.8 %custom-call.13 = f32[1,128,128]{1,2,0:T(8,128)S(1)} custom-call(f32[1,128,128]{2,1,0:T(8,128)S(1)} %get-tuple-element.79), custom_call_target="InvertDiagBlocksLowerTriangular" | custom-call | tf_op jit(solution)/shard_map/jit(cholesky)/cholesky | solution.py:91
  98.4 11.7 %cholesky.147 = f32[128,128]{1,0:T(8,128)S(1)} custom-call(f32[128,128]{1,0:T(8,128)S(1)} %convolution_subtract_fusion.6), custom_call_target="Cholesky" | custom-call | tf_op jit(solution)/shard_map/jit(cholesky)/cholesky | solution.py:91
  110.1 0.7 compare_reduce_fusion.2
  110.8 0.7 compare_reduce_fusion.3
  112.9 15.5 %while.4 = (s32[]{:T(128)}, f32[256,256]{1,0:T(8,128)S(1)}, s32[2,2]{1,0:T(2,128)S(1)}, f32[2,128,128]{2,1,0:T(8,128)S(1)}, s32[]{:T(128)}) while((s32[]{:T(128)}, f32[256,256]{1,0:T(8,128)S(1)}, s32[2,2]{1,0:T(2,128)S(1)}, f32[2,128,128]{2,1,0:T(8,128)S(1)}, s32[]{:T(128)}) %tuple.77), condition=%wide.while_cond, body=%wide.while_body.sunk | while | flops 2 | bytes 131181 | solution.py:92
  125.1 1.4 bitcast_dynamic-update-slice_fusion.4
  127.0 1.4 bitcast_dynamic-update-slice_fusion.4
  128.4 19.7 %custom-call.14 = f32[2,128,128]{1,2,0:T(8,128)S(1)} custom-call(f32[2,128,128]{2,1,0:T(8,128)S(1)} %get-tuple-element.22), custom_call_target="InvertDiagBlocksLowerTriangular" | custom-call | tf_op jit(solution)/shard_map/jit(_solve_triangular)/triangular_solve | solution.py:92
  148.2 1.7 fusion.2
  150.9 0.8 fusion.15
  152.1 0.7 gather_fusion.1
  152.9 0.7 select_select_fusion.2
  154.5 39.7 %all_gather.14 = bf16[1024,384]{1,0:T(8,128)(2,1)S(1)} all-gather(bf16[32,384]{1,0:T(8,128)(2,1)S(1)} %select_select_fusion.4), channel_id=1, replica_groups=mesh['rows'=16,'feat'=2] {'rows','feat'}, dimensions={0}, use_global_device_ids=true | all-gather | bytes 811008 | tf_op jit(solution)/shard_map/all_gather | solution.py:47
  194.2 1.2 gather_fusion.9
  195.4 1.2 gather_fusion.8
  196.8 1.3 convolution_bitcast_fusion
  198.2 1.0 fusion.9
  199.9 7.0 %all-gather.5.cloned.1.call-done = f32[1024,512]{1,0:T(8,128)} async-done(((f32[32,512]{1,0:T(8,128)}), f32[1024,512]{1,0:T(8,128)}) %all-gather.5.cloned.1.call-update) | async-done | bytes 2097168 | tf_op jit(solution)/shard_map/all_gather | solution.py:48
  206.9 2.9 %gather_fusion.10 = f32[256,512]{1,0:T(8,128)S(1)} fusion(f32[1024,512]{1,0:T(8,128)} %all-gather.5.cloned.1.call-done, s32[1024]{0:T(1024)S(1)} %pad_clamp_fusion.2), kind=kCustom, calls=%fused_computation.3.clone | custom fusion | bytes 1049600 | tf_op jit(solution)/shard_map/jit(_take)/gather | solution.py:55
  209.8 1.0 gather_fusion.11
  210.8 1.8 convolution_subtract_fusion.2
  212.8 11.7 %cholesky.164 = f32[128,128]{1,0:T(8,128)S(1)} custom-call(f32[128,128]{1,0:T(8,128)S(1)} %cholesky.197), custom_call_target="Cholesky" | custom-call | tf_op jit(solution)/shard_map/jit(cholesky)/cholesky | solution.py:91
  224.6 9.8 %custom-call.15 = f32[1,128,128]{1,2,0:T(8,128)S(1)} custom-call(f32[1,128,128]{2,1,0:T(8,128)S(1)} %get-tuple-element.75), custom_call_target="InvertDiagBlocksLowerTriangular" | custom-call | tf_op jit(solution)/shard_map/jit(cholesky)/cholesky | solution.py:91
  234.9 11.9 %cholesky.181 = f32[128,128]{1,0:T(8,128)S(1)} custom-call(f32[128,128]{1,0:T(8,128)S(1)} %convolution_subtract_fusion.5), custom_call_target="Cholesky" | custom-call | tf_op jit(solution)/shard_map/jit(cholesky)/cholesky | solution.py:91
  246.8 0.7 compare_reduce_fusion
  247.5 0.6 compare_reduce_fusion.1
  249.4 3.9 %while.5 = (s32[]{:T(128)}, f32[256,256]{1,0:T(8,128)S(1)}, s32[2,2]{1,0:T(2,128)S(1)}, f32[2,128,128]{2,1,0:T(8,128)S(1)}, s32[]{:T(128)}) while((s32[]{:T(128)}, f32[256,256]{1,0:T(8,128)S(1)}, s32[2,2]{1,0:T(2,128)S(1)}, f32[2,128,128]{2,1,0:T(8,128)S(1)}, s32[]{:T(128)}) %tuple.91), condition=%wide.while_cond.clone, body=%wide.while_body.clone.sunk | while | flops 2 | bytes 131181 | solution.py:92
  249.4 0.6 fusion.71
  250.0 1.3 bitcast_dynamic-update-slice_fusion.5
  251.3 0.6 fusion.71
  252.0 1.3 bitcast_dynamic-update-slice_fusion.5
  253.3 19.7 %custom-call.16 = f32[2,128,128]{1,2,0:T(8,128)S(1)} custom-call(f32[2,128,128]{2,1,0:T(8,128)S(1)} %get-tuple-element.23), custom_call_target="InvertDiagBlocksLowerTriangular" | custom-call | tf_op jit(solution)/shard_map/jit(_solve_triangular)/triangular_solve | solution.py:92
  273.0 2.1 fusion
  276.5 1.1 copy.35
  (160 shorter events, 13.5 us)
Async XLA Ops:
  8.0 64.3 %all-gather.3.cloned.1.call-start = ((), (), s32[]{:S(2)}) async-start(), calls=%async_computation.2 | async-start | bytes 1081344 | tf_op jit(solution)/shard_map/all_gather | solution.py:48
  9.6 55.4 %copy-start.9 = (s32[256]{0:T(256)}, s32[256]{0:T(256)S(1)}, u32[]{:S(2)}) copy-start(s32[256]{0:T(256)S(1)} %get-tuple-element.96) | copy-start | bytes 3076
  12.4 135.7 %reduce-scatter.3.cloned.1.call-start = ((), (), s32[]{:S(2)}) async-start(), calls=%async_computation.3 | async-start | bytes 1179648 | tf_op jit(solution)/shard_map/reduce_scatter | solution.py:62
  14.3 61.2 %copy-start.11 = (pred[256]{0:T(512)(128)(4,1)}, pred[256]{0:T(512)(128)(4,1)S(1)}, u32[]{:S(2)}) copy-start(pred[256]{0:T(512)(128)(4,1)S(1)} %get-tuple-element.58) | copy-start | bytes 772
  14.3 61.2 %copy-start.13 = (pred[256]{0:T(512)(128)(4,1)}, pred[256]{0:T(512)(128)(4,1)S(1)}, u32[]{:S(2)}) copy-start(pred[256]{0:T(512)(128)(4,1)S(1)} %get-tuple-element.80) | copy-start | bytes 772
  60.1 2.6 copy-start.2
  62.4 2.5 copy-start.5
  63.9 7.0 %copy-start.31 = (u32[32]{0:T(128)S(1)}, u32[32]{0:T(128)}, u32[]{:S(2)}) copy-start(u32[32]{0:T(128)} %constant.204) | copy-start | bytes 388
  63.9 142.9 %all-gather.5.cloned.1.call-start = ((), (), s32[]{:S(2)}) async-start(), calls=%async_computation.4 | async-start | bytes 2162688 | tf_op jit(solution)/shard_map/all_gather | solution.py:48
  64.2 8.1 %copy-start.20 = (f32[256]{0:T(256)}, f32[256]{0:T(256)S(1)}, u32[]{:S(2)}) copy-start(f32[256]{0:T(256)S(1)} %multiply_reduce_fusion.2) | copy-start | bytes 3076
  65.2 1.9 copy-start.7
  72.3 2.3 copy-start.1
  75.5 37.2 %copy-start.32 = (s32[2]{0:T(128)S(1)}, s32[2]{0:T(128)}, u32[]{:S(2)}) copy-start(s32[2]{0:T(128)} %iota_multiply_fusion) | copy-start | bytes 28
  76.1 72.1 %copy-start.12 = (pred[256]{0:T(512)(128)(4,1)S(1)}, pred[256]{0:T(512)(128)(4,1)}, u32[]{:S(2)}) copy-start(pred[256]{0:T(512)(128)(4,1)} %copy-done.11) | copy-start | bytes 772
  76.1 72.1 %copy-start.14 = (pred[256]{0:T(512)(128)(4,1)S(1)}, pred[256]{0:T(512)(128)(4,1)}, u32[]{:S(2)}) copy-start(pred[256]{0:T(512)(128)(4,1)} %copy-done.13) | copy-start | bytes 772
  76.1 72.1 %copy-start.21 = (f32[256]{0:T(256)S(1)}, f32[256]{0:T(256)}, u32[]{:S(2)}) copy-start(f32[256]{0:T(256)} %copy-done.20) | copy-start | bytes 3076
  128.4 21.8 %copy-start.29 = (s32[2,2]{1,0:T(2,128)}, s32[2,2]{1,0:T(2,128)S(1)}, u32[]{:S(2)}) copy-start(s32[2,2]{1,0:T(2,128)S(1)} %get-tuple-element.204) | copy-start | bytes 52
  151.7 2.7 copy-start.3
  151.7 1.1 copy-start.25
  151.8 1.1 copy-start.27
  151.8 1.9 copy-start.28
  151.8 2.6 copy-start.8
  151.8 2.5 copy-start.10
  151.8 2.6 copy-start.24
  153.6 119.4 %reduce-scatter.5.cloned.1.call-start = ((), (), s32[]{:S(2)}) async-start(), calls=%async_computation.5 | async-start | bytes 1179648 | tf_op jit(solution)/shard_map/reduce_scatter | solution.py:62
  154.3 42.2 %copy-start.16 = (pred[256]{0:T(512)(128)(4,1)}, pred[256]{0:T(512)(128)(4,1)S(1)}, u32[]{:S(2)}) copy-start(pred[256]{0:T(512)(128)(4,1)S(1)} %get-tuple-element.62) | copy-start | bytes 772
  154.4 42.3 %copy-start.18 = (pred[256]{0:T(512)(128)(4,1)}, pred[256]{0:T(512)(128)(4,1)S(1)}, u32[]{:S(2)}) copy-start(pred[256]{0:T(512)(128)(4,1)S(1)} %get-tuple-element.90) | copy-start | bytes 772
  198.2 8.6 %copy-start.22 = (f32[256]{0:T(256)}, f32[256]{0:T(256)S(1)}, u32[]{:S(2)}) copy-start(f32[256]{0:T(256)S(1)} %multiply_reduce_fusion.1) | copy-start | bytes 3076
  206.9 3.0 %copy-start = (f32[1024,512]{1,0:T(8,128)S(1)}, f32[1024,512]{1,0:T(8,128)}, u32[]{:S(2)}) copy-start(f32[1024,512]{1,0:T(8,128)} %all-gather.5.cloned.1.call-done) | copy-start | bytes 6291460
  210.8 38.6 %copy-start.30 = (s32[2,2]{1,0:T(2,128)S(1)}, s32[2,2]{1,0:T(2,128)}, u32[]{:S(2)}) copy-start(s32[2,2]{1,0:T(2,128)} %copy-done.29) | copy-start | bytes 52
  212.6 60.4 %copy-start.4 = (f32[384,256]{0,1:T(8,128)S(1)}, f32[384,256]{0,1:T(8,128)}, u32[]{:S(2)}) copy-start(f32[384,256]{0,1:T(8,128)} %copy-done.3) | copy-start | bytes 1179652
  212.6 60.4 %copy-start.17 = (pred[256]{0:T(512)(128)(4,1)S(1)}, pred[256]{0:T(512)(128)(4,1)}, u32[]{:S(2)}) copy-start(pred[256]{0:T(512)(128)(4,1)} %copy-done.16) | copy-start | bytes 772
  212.6 60.4 %copy-start.19 = (pred[256]{0:T(512)(128)(4,1)S(1)}, pred[256]{0:T(512)(128)(4,1)}, u32[]{:S(2)}) copy-start(pred[256]{0:T(512)(128)(4,1)} %copy-done.18) | copy-start | bytes 772
  212.6 60.4 %copy-start.23 = (f32[256]{0:T(256)S(1)}, f32[256]{0:T(256)}, u32[]{:S(2)}) copy-start(f32[256]{0:T(256)} %copy-done.22) | copy-start | bytes 3076
  273.0 3.4 %copy-start.6 = (f32[1,384,256]{1,2,0:T(8,128)S(1)}, f32[1,384,256]{1,2,0:T(8,128)}, u32[]{:S(2)}) copy-start(f32[1,384,256]{1,2,0:T(8,128)} %get-tuple-element.70) | copy-start | bytes 1179652
  276.3 1.3 copy-start.15
  276.3 1.3 copy-start.26
Sparse Core Ops, SparseCore 0:
  12.6 57.0 all-gather.2
  153.7 53.1 all-gather.4
Sparse Core Ops, SparseCore 1:
  64.0 4.2 reduce-scatter.2
  198.2 5.6 reduce-scatter.4
where the time goes:
time: 290 us; the launch traced here: 286 us
  other arithmetic  119 us (41%)
  blocking collectives  88.1 us (30%)
  local copies, waits for them, and re-layouts  27.1 us (9%)
  between operations  19.7 us (7%)
  matrix products  13.1 us (5%)
  loops' own time  11.6 us (4%)
  waiting for transfers between devices  7.08 us (2%)
    all_gather x2, blocking collectives, shards(): all_x = lax.all_gather(packed_x, ('rows', 'feat'), axis=0, tiled=True)  85.3 us
    another operation x14, other arithmetic, shards(): chol_lower = jnp.linalg.cholesky(pivot_block)  69.4 us
    another operation x5, other arithmetic, shards(): jax.scipy.linalg.solve_triangular(chol_lower, kernel_panel.T, lower=True)  39.9 us
    another operation x2, loops' own time, shards(): jax.scipy.linalg.solve_triangular(chol_lower, kernel_panel.T, lower=True)  11.6 us
    another operation x15, local copies, waits for them, and re-layouts, shards(): jax.scipy.linalg.solve_triangular(chol_lower, kernel_panel.T, lower=True)  7.88 us
    gather x4, local copies, waits for them, and re-layouts, shards(): pivot_factor = pivot_factor + jnp.take(all_f, source, axis=0)  7.17 us
    all_gather x2, waiting for transfers between devices, shards(): all_f = lax.all_gather(packed_f, ('rows', 'feat'), axis=0, tiled=True)  6.96 us
  transfers between devices with their start and end apart: 4, of which 1 were waited for; matrix products, arithmetic and copies ran while one was open for 50% of the time, Pallas kernels for 0%

commit v1 on v0

--- a/solution.py
+++ b/solution.py
@@ -44,7 +44,26 @@
         slot_half_rows = jnp.sum(jnp.where(half_hits, half_safe[None, :], 0), axis=1)
         packed_x = jnp.where(slot_full[:, None], jnp.take(embeddings, slot_rows, axis=0), 0)
         packed_f = jnp.where(slot_half[:, None], jnp.take(current, slot_half_rows, axis=0), 0.0)
-        all_x = lax.all_gather(packed_x, ("rows", "feat"), axis=0, tiled=True)
+        t_next, now, current_block = (
+            lax.axis_size(("rows", "feat")),
+            lax.axis_index(("rows", "feat")),
+            packed_x.shape[0],
+        )
+        fresh, wide_out = (packed_x, 1)
+        while wide_out < t_next:
+            fresh = jnp.concatenate(
+                [
+                    fresh,
+                    lax.ppermute(
+                        fresh,
+                        ("rows", "feat"),
+                        [(at, (at - wide_out) % t_next) for at in range(t_next)],
+                    ),
+                ],
+                axis=0,
+            )
+            wide_out = 2 * wide_out
+        all_x = jnp.roll(fresh, shift=now * current_block, axis=0)
         all_f = lax.all_gather(packed_f, ("rows", "feat"), axis=0, tiled=True)
         first_src = owners * feat_count * capacity + pivot_ranks
         pieces = []

time: 290 us -> 314 us (1.083)
  waiting for transfers between devices: 7.08 us -> 100 us
  blocking collectives: 88.1 us -> 2.47 us
  starting transfers between devices: 0.17 us -> 16.8 us
  loops' own time: 11.6 us -> 0.1 us
  local copies, waits for them, and re-layouts: 27.1 us -> 35 us
    all_gather x2 -> x0, blocking collectives: 85.3 us -> none  [shards(): all_x = lax.all_gather(packed_x, ('rows', 'feat'), axis=0, tiled=True)]
    ppermute x0 -> x10, waiting for transfers between devices: none -> 46.7 us  [shards(): lax.ppermute(fresh, ('rows', 'feat'), [(at, (at - wide_out) % t_next) for...]
    all_gather x2, waiting for transfers between devices: 6.96 us -> 53.1 us  [shards(): all_f = lax.all_gather(packed_f, ('rows', 'feat'), axis=0, tiled=True)]
    ppermute x0 -> x10, starting transfers between devices: none -> 16 us  [shards(): lax.ppermute(fresh, ('rows', 'feat'), [(at, (at - wide_out) % t_next) for...]
    another operation x2, loops' own time: 11.6 us -> 0.1 us  [shards(): jax.scipy.linalg.solve_triangular(chol_lower, kernel_panel.T, lower=True)]
  transfers between devices with their start and end apart: 4 -> 14, of which waited for: 1 -> 7; matrix products, arithmetic and copies ran while one was open for 50% -> 49% of each run, Pallas kernels for 0% -> 0%
where the time goes in v1:
time: 314 us; the launch traced here: 308 us
  other arithmetic  120 us (38%)
  waiting for transfers between devices  100 us (32%)
  local copies, waits for them, and re-layouts  35 us (11%)
  between operations  19.7 us (6%)
  starting transfers between devices  16.8 us (5%)
  matrix products  14.8 us (5%)
    another operation x14, other arithmetic, shards(): chol_lower = jnp.linalg.cholesky(pivot_block)  69.4 us
    all_gather x2, waiting for transfers between devices, shards(): all_f = lax.all_gather(packed_f, ('rows', 'feat'), axis=0, tiled=True)  53.1 us
    ppermute x10, waiting for transfers between devices, shards(): lax.ppermute(fresh, ('rows', 'feat'), [(at, (at - wide_out) % t_next) for...  46.7 us
    another operation x5, other arithmetic, shards(): jax.scipy.linalg.solve_triangular(chol_lower, kernel_panel.T, lower=True)  39.4 us
    ppermute x10, starting transfers between devices, shards(): lax.ppermute(fresh, ('rows', 'feat'), [(at, (at - wide_out) % t_next) for...  16 us
    gather x4, local copies, waits for them, and re-layouts, shards(): pivot_factor = pivot_factor + jnp.take(all_f, source, axis=0)  7.99 us
    another operation x15, local copies, waits for them, and re-layouts, shards(): jax.scipy.linalg.solve_triangular(chol_lower, kernel_panel.T, lower=True)  7.66 us
  transfers between devices with their start and end apart: 14, of which 7 were waited for; matrix products, arithmetic and copies ran while one was open for 49% of the time, Pallas kernels for 0%

profile of v1, /device:TPU:0, one launch (start us, length us, event | category | flops | bytes accessed | tf_op | source)
XLA Modules:
  0.0 308.4 jit_solution(13876025045779841711)
XLA Ops:
  10.5 1.6 gather_fusion
  12.8 1.8 gather_fusion.2
  14.7 6.5 %collective-permute-start = (bf16[32,384]{1,0:T(8,128)(2,1)S(1)}, bf16[32,384]{1,0:T(8,128)(2,1)S(1)}, u32[]{:S(2)}, u32[]{:S(2)}) collective-permute-start(bf16[32,384]{1,0:T(8,128)(2,1)S(1)} %get-tuple-element.64), channel_id=1, source_target_pairs={{0,31},{1,0},{2,1},{3,2},{4,3},{5,4},{6,5},{7,6},{8,7},{9,8},{10,9... | collective-permute-start | bytes 73736 | tf_op jit(solution)/shard_map/ppermute | solution.py:57
  21.3 1.8 gather_fusion.7
  23.9 1.3 multiply_reduce_fusion
  26.4 1.5 collective-permute-start.6
  28.5 1.4 collective-permute-done.1
  31.0 1.3 collective-permute-start.7
  32.9 2.1 collective-permute-done.2
  35.0 1.2 collective-permute-start.3
  38.2 9.1 %collective-permute-done.8 = bf16[256,384]{1,0:T(8,128)(2,1)S(1)} collective-permute-done((bf16[256,384]{1,0:T(8,128)(2,1)S(1)}, bf16[256,384]{1,0:T(8,128)(2,1)S(1)}, u32[]{:S(2)}, u32[]{:S(2)}) %collective-permute-start.8) | collective-permute-done | bytes 196640 | tf_op jit(solution)/shard_map/ppermute | solution.py:57
  48.2 2.9 collective-permute-start.4
  52.5 2.5 all-reduce.1
  55.1 22.9 %collective-permute-done.9 = bf16[512,384]{1,0:T(8,128)(2,1)S(1)} collective-permute-done((bf16[512,384]{1,0:T(8,128)(2,1)S(1)}, bf16[512,384]{1,0:T(8,128)(2,1)S(1)}, u32[]{:S(2)}, u32[]{:S(2)}) %collective-permute-start.9) | collective-permute-done | bytes 393248 | tf_op jit(solution)/shard_map/ppermute | solution.py:57
  78.1 10.2 %collective-permute-done.4 = bf16[512,384]{1,0:T(8,128)(2,1)S(1)} collective-permute-done((bf16[512,384]{1,0:T(8,128)(2,1)S(1)}, bf16[512,384]{1,0:T(8,128)(2,1)S(1)}, u32[]{:S(2)}, u32[]{:S(2)}) %collective-permute-start.4) | collective-permute-done | bytes 393248 | tf_op jit(solution)/shard_map/ppermute | solution.py:57
  89.2 2.3 fusion.13
  91.4 1.2 gather_fusion.3
  92.6 1.2 gather_fusion.4
  95.2 1.3 convolution_bitcast_fusion.1
  97.0 2.3 gather_fusion.6
  99.3 1.7 gather_fusion.5
  101.0 1.6 convolution_subtract_fusion.1
  102.8 11.7 %cholesky.130 = f32[128,128]{1,0:T(8,128)S(1)} custom-call(f32[128,128]{1,0:T(8,128)S(1)} %cholesky.194), custom_call_target="Cholesky" | custom-call | tf_op jit(solution)/shard_map/jit(cholesky)/cholesky | solution.py:110
  114.6 9.8 %custom-call.13 = f32[1,128,128]{1,2,0:T(8,128)S(1)} custom-call(f32[1,128,128]{2,1,0:T(8,128)S(1)} %get-tuple-element.92), custom_call_target="InvertDiagBlocksLowerTriangular" | custom-call | tf_op jit(solution)/shard_map/jit(cholesky)/cholesky | solution.py:110
  124.9 11.7 %cholesky.147 = f32[128,128]{1,0:T(8,128)S(1)} custom-call(f32[128,128]{1,0:T(8,128)S(1)} %convolution_subtract_fusion.6), custom_call_target="Cholesky" | custom-call | tf_op jit(solution)/shard_map/jit(cholesky)/cholesky | solution.py:110
  139.3 4.0 %while.4 = (s32[]{:T(128)}, f32[256,256]{1,0:T(8,128)S(1)}, s32[2,2]{1,0:T(2,128)S(1)}, f32[2,128,128]{2,1,0:T(8,128)S(1)}, s32[]{:T(128)}) while((s32[]{:T(128)}, f32[256,256]{1,0:T(8,128)S(1)}, s32[2,2]{1,0:T(2,128)S(1)}, f32[2,128,128]{2,1,0:T(8,128)S(1)}, s32[]{:T(128)}) %tuple.92), condition=%wide.while_cond, body=%wide.while_body.sunk | while | flops 2 | bytes 131189 | solution.py:111
  140.0 1.4 bitcast_dynamic-update-slice_fusion.4
  141.9 1.4 bitcast_dynamic-update-slice_fusion.4
  143.3 19.7 %custom-call.14 = f32[2,128,128]{1,2,0:T(8,128)S(1)} custom-call(f32[2,128,128]{2,1,0:T(8,128)S(1)} %get-tuple-element.23), custom_call_target="InvertDiagBlocksLowerTriangular" | custom-call | tf_op jit(solution)/shard_map/jit(_solve_triangular)/triangular_solve | solution.py:111
  163.1 1.7 fusion.2
  166.7 1.1 copy.31
  167.9 1.8 gather_fusion.1
  170.6 1.2 gather_fusion.8
  171.8 1.2 gather_fusion.9
  173.4 1.0 fusion.9
  174.4 1.3 convolution_bitcast_fusion
  176.4 53.1 %all-gather.5.cloned.1.call-done = f32[1024,512]{1,0:T(8,128)} async-done(((f32[32,512]{1,0:T(8,128)}), f32[1024,512]{1,0:T(8,128)}) %all-gather.5.cloned.1.call-update) | async-done | bytes 2097168 | tf_op jit(solution)/shard_map/all_gather | solution.py:67
  229.5 3.1 %gather_fusion.11 = f32[256,512]{1,0:T(8,128)S(1)} fusion(f32[1024,512]{1,0:T(8,128)} %all-gather.5.cloned.1.call-done, s32[1024]{0:T(1024)} %copy-done.9), kind=kCustom, calls=%fused_computation.9.clone | custom fusion | bytes 1049600 | tf_op jit(solution)/shard_map/jit(_take)/gather | solution.py:74
  233.5 1.8 convolution_subtract_fusion.2
  235.5 11.7 %cholesky.164 = f32[128,128]{1,0:T(8,128)S(1)} custom-call(f32[128,128]{1,0:T(8,128)S(1)} %cholesky.197), custom_call_target="Cholesky" | custom-call | tf_op jit(solution)/shard_map/jit(cholesky)/cholesky | solution.py:110
  247.3 9.8 %custom-call.15 = f32[1,128,128]{1,2,0:T(8,128)S(1)} custom-call(f32[1,128,128]{2,1,0:T(8,128)S(1)} %get-tuple-element.88), custom_call_target="InvertDiagBlocksLowerTriangular" | custom-call | tf_op jit(solution)/shard_map/jit(cholesky)/cholesky | solution.py:110
  257.6 11.9 %cholesky.181 = f32[128,128]{1,0:T(8,128)S(1)} custom-call(f32[128,128]{1,0:T(8,128)S(1)} %convolution_subtract_fusion.5), custom_call_target="Cholesky" | custom-call | tf_op jit(solution)/shard_map/jit(cholesky)/cholesky | solution.py:110
  272.1 3.7 %while.5 = (s32[]{:T(128)}, f32[256,256]{1,0:T(8,128)S(1)}, s32[2,2]{1,0:T(2,128)S(1)}, f32[2,128,128]{2,1,0:T(8,128)S(1)}, s32[]{:T(128)}) while((s32[]{:T(128)}, f32[256,256]{1,0:T(8,128)S(1)}, s32[2,2]{1,0:T(2,128)S(1)}, f32[2,128,128]{2,1,0:T(8,128)S(1)}, s32[]{:T(128)}) %tuple.106), condition=%wide.while_cond.clone, body=%wide.while_body.clone.sunk | while | flops 2 | bytes 131189 | solution.py:111
  272.7 1.2 bitcast_dynamic-update-slice_fusion.5
  274.6 1.2 bitcast_dynamic-update-slice_fusion.5
  275.8 19.7 %custom-call.16 = f32[2,128,128]{1,2,0:T(8,128)S(1)} custom-call(f32[2,128,128]{2,1,0:T(8,128)S(1)} %get-tuple-element.24), custom_call_target="InvertDiagBlocksLowerTriangular" | custom-call | tf_op jit(solution)/shard_map/jit(_solve_triangular)/triangular_solve | solution.py:111
  295.6 2.1 fusion
  299.0 1.1 copy.35
  (170 shorter events, 27.5 us)
Async XLA Ops:
  8.0 89.0 %all-gather.3.cloned.1.call-start = ((), (), s32[]{:S(2)}) async-start(), calls=%async_computation.2 | async-start | bytes 1081344 | tf_op jit(solution)/shard_map/all_gather | solution.py:67
  12.8 150.3 %reduce-scatter.3.cloned.1.call-start = ((), (), s32[]{:S(2)}) async-start(), calls=%async_computation.3 | async-start | bytes 1179648 | tf_op jit(solution)/shard_map/reduce_scatter | solution.py:81
  14.7 11.1 %collective-permute-start = (bf16[32,384]{1,0:T(8,128)(2,1)S(1)}, bf16[32,384]{1,0:T(8,128)(2,1)S(1)}, u32[]{:S(2)}, u32[]{:S(2)}) collective-permute-start(bf16[32,384]{1,0:T(8,128)(2,1)S(1)} %get-tuple-element.64), channel_id=1, source_target_pairs={{0,31},{1,0},{2,1},{3,2},{4,3},{5,4},{6,5},{7,6},{8,7},{9,8},{10,9... | collective-permute-start | bytes 73736 | tf_op jit(solution)/shard_map/ppermute | solution.py:57
  23.2 3.2 %collective-permute-start.5 = (bf16[32,384]{1,0:T(8,128)(2,1)S(1)}, bf16[32,384]{1,0:T(8,128)(2,1)S(1)}, u32[]{:S(2)}, u32[]{:S(2)}) collective-permute-start(bf16[32,384]{1,0:T(8,128)(2,1)S(1)} %get-tuple-element.70), channel_id=1, source_target_pairs={{0,31},{1,0},{2,1},{3,2},{4,3},{5,4},{6,5},{7,6},{8,7},{9,8},{10,9... | collective-permute-start | bytes 73736 | tf_op jit(solution)/shard_map/ppermute | solution.py:57
  25.8 4.1 %collective-permute-start.1 = (bf16[64,384]{1,0:T(8,128)(2,1)S(1)}, bf16[64,384]{1,0:T(8,128)(2,1)S(1)}, u32[]{:S(2)}, u32[]{:S(2)}) collective-permute-start(bf16[64,384]{1,0:T(8,128)(2,1)S(1)} %pad_maximum_fusion.12), channel_id=1, source_target_pairs={{0,30},{1,31},{2,0},{3,1},{4,2},{5,3},{6,4},{7,5},{8,6},{9,7},{10,... | collective-permute-start | bytes 147464 | tf_op jit(solution)/shard_map/ppermute | solution.py:57
  26.4 4.5 %collective-permute-start.6 = (bf16[64,384]{1,0:T(8,128)(2,1)S(1)}, bf16[64,384]{1,0:T(8,128)(2,1)S(1)}, u32[]{:S(2)}, u32[]{:S(2)}) collective-permute-start(bf16[64,384]{1,0:T(8,128)(2,1)S(1)} %pad_maximum_fusion.13), channel_id=1, source_target_pairs={{0,30},{1,31},{2,0},{3,1},{4,2},{5,3},{6,4},{7,5},{8,6},{9,7},{10,... | collective-permute-start | bytes 147464 | tf_op jit(solution)/shard_map/ppermute | solution.py:57
  30.0 21.1 %copy-start.5 = (f32[384,256]{1,0:T(8,128)S(1)}, f32[384,256]{1,0:T(8,128)}, u32[]{:S(2)}) copy-start(f32[384,256]{1,0:T(8,128)} %param.18) | copy-start | bytes 1179652
  30.0 5.0 %collective-permute-start.2 = (bf16[128,384]{1,0:T(8,128)(2,1)S(1)}, bf16[128,384]{1,0:T(8,128)(2,1)S(1)}, u32[]{:S(2)}, u32[]{:S(2)}) collective-permute-start(bf16[128,384]{1,0:T(8,128)(2,1)S(1)} %pad_maximum_fusion.10), channel_id=1, source_target_pairs={{0,28},{1,29},{2,30},{3,31},{4,0},{5,1},{6,2},{7,3},{8,4},{9,5},{1... | collective-permute-start | bytes 294920 | tf_op jit(solution)/shard_map/ppermute | solution.py:57
  31.0 6.1 %collective-permute-start.7 = (bf16[128,384]{1,0:T(8,128)(2,1)S(1)}, bf16[128,384]{1,0:T(8,128)(2,1)S(1)}, u32[]{:S(2)}, u32[]{:S(2)}) collective-permute-start(bf16[128,384]{1,0:T(8,128)(2,1)S(1)} %pad_maximum_fusion.11), channel_id=1, source_target_pairs={{0,28},{1,29},{2,30},{3,31},{4,0},{5,1},{6,2},{7,3},{8,4},{9,5},{1... | collective-permute-start | bytes 294920 | tf_op jit(solution)/shard_map/ppermute | solution.py:57
  35.0 16.3 %copy-start.20 = (u32[32]{0:T(128)S(1)}, u32[32]{0:T(128)}, u32[]{:S(2)}) copy-start(u32[32]{0:T(128)} %constant.224) | copy-start | bytes 388
  35.0 12.4 %collective-permute-start.3 = (bf16[256,384]{1,0:T(8,128)(2,1)S(1)}, bf16[256,384]{1,0:T(8,128)(2,1)S(1)}, u32[]{:S(2)}, u32[]{:S(2)}) collective-permute-start(bf16[256,384]{1,0:T(8,128)(2,1)S(1)} %pad_maximum_fusion.8), channel_id=1, source_target_pairs={{0,24},{1,25},{2,26},{3,27},{4,28},{5,29},{6,30},{7,31},{8,0},{9,1... | collective-permute-start | bytes 589832 | tf_op jit(solution)/shard_map/ppermute | solution.py:57
  37.1 10.2 %collective-permute-start.8 = (bf16[256,384]{1,0:T(8,128)(2,1)S(1)}, bf16[256,384]{1,0:T(8,128)(2,1)S(1)}, u32[]{:S(2)}, u32[]{:S(2)}) collective-permute-start(bf16[256,384]{1,0:T(8,128)(2,1)S(1)} %pad_maximum_fusion.9), channel_id=1, source_target_pairs={{0,24},{1,25},{2,26},{3,27},{4,28},{5,29},{6,30},{7,31},{8,0},{9,1... | collective-permute-start | bytes 589832 | tf_op jit(solution)/shard_map/ppermute | solution.py:57
  47.4 30.6 %collective-permute-start.9 = (bf16[512,384]{1,0:T(8,128)(2,1)S(1)}, bf16[512,384]{1,0:T(8,128)(2,1)S(1)}, u32[]{:S(2)}, u32[]{:S(2)}) collective-permute-start(bf16[512,384]{1,0:T(8,128)(2,1)S(1)} %get-tuple-element.79), channel_id=1, source_target_pairs={{0,16},{1,17},{2,18},{3,19},{4,20},{5,21},{6,22},{7,23},{8,24},{9,... | collective-permute-start | bytes 1179656 | tf_op jit(solution)/shard_map/ppermute | solution.py:57
  48.2 40.1 %collective-permute-start.4 = (bf16[512,384]{1,0:T(8,128)(2,1)S(1)}, bf16[512,384]{1,0:T(8,128)(2,1)S(1)}, u32[]{:S(2)}, u32[]{:S(2)}) collective-permute-start(bf16[512,384]{1,0:T(8,128)(2,1)S(1)} %get-tuple-element.77), channel_id=1, source_target_pairs={{0,16},{1,17},{2,18},{3,19},{4,20},{5,21},{6,22},{7,23},{8,24},{9,... | collective-permute-start | bytes 1179656 | tf_op jit(solution)/shard_map/ppermute | solution.py:57
  78.1 10.3 %copy-start.8 = (bf16[1024,384]{1,0:T(8,128)(2,1)}, bf16[1024,384]{1,0:T(8,128)(2,1)S(1)}, u32[]{:S(2)}) copy-start(bf16[1024,384]{1,0:T(8,128)(2,1)S(1)} %constant_dynamic-update-slice_fusion.16) | copy-start | bytes 2359300
  93.8 1.4 copy-start.2
  96.5 133.0 %all-gather.5.cloned.1.call-start = ((), (), s32[]{:S(2)}) async-start(), calls=%async_computation.4 | async-start | bytes 2162688 | tf_op jit(solution)/shard_map/all_gather | solution.py:67
  97.0 2.3 copy-start.1
  102.8 60.3 %copy-start.6 = (f32[256,256]{1,0:T(8,128)S(1)}, f32[256,256]{1,0:T(8,128)}, u32[]{:S(2)}) copy-start(f32[256,256]{1,0:T(8,128)} %gather_fusion.5) | copy-start | bytes 786436
  143.3 22.5 %copy-start.18 = (s32[2,2]{1,0:T(2,128)}, s32[2,2]{1,0:T(2,128)S(1)}, u32[]{:S(2)}) copy-start(s32[2,2]{1,0:T(2,128)S(1)} %get-tuple-element.253) | copy-start | bytes 52
  166.6 1.2 copy-start.3
  170.3 125.2 %reduce-scatter.5.cloned.1.call-start = ((), (), s32[]{:S(2)}) async-start(), calls=%async_computation.5 | async-start | bytes 1179648 | tf_op jit(solution)/shard_map/reduce_scatter | solution.py:81
  170.6 2.4 copy-start.11
  170.6 2.5 copy-start.13
  170.6 2.3 copy-start.9
  173.4 2.3 copy-start.15
  229.5 3.1 %copy-start = (f32[1024,512]{1,0:T(8,128)S(1)}, f32[1024,512]{1,0:T(8,128)}, u32[]{:S(2)}) copy-start(f32[1024,512]{1,0:T(8,128)} %all-gather.5.cloned.1.call-done) | copy-start | bytes 6291460
  235.3 36.8 %copy-start.19 = (s32[2,2]{1,0:T(2,128)S(1)}, s32[2,2]{1,0:T(2,128)}, u32[]{:S(2)}) copy-start(s32[2,2]{1,0:T(2,128)} %copy-done.18) | copy-start | bytes 52
  235.5 60.1 %copy-start.4 = (f32[384,256]{0,1:T(8,128)S(1)}, f32[384,256]{0,1:T(8,128)}, u32[]{:S(2)}) copy-start(f32[384,256]{0,1:T(8,128)} %copy-done.3) | copy-start | bytes 1179652
  235.5 60.1 %copy-start.12 = (pred[256]{0:T(512)(128)(4,1)S(1)}, pred[256]{0:T(512)(128)(4,1)}, u32[]{:S(2)}) copy-start(pred[256]{0:T(512)(128)(4,1)} %copy-done.11) | copy-start | bytes 772
  235.5 60.1 %copy-start.14 = (pred[256]{0:T(512)(128)(4,1)S(1)}, pred[256]{0:T(512)(128)(4,1)}, u32[]{:S(2)}) copy-start(pred[256]{0:T(512)(128)(4,1)} %copy-done.13) | copy-start | bytes 772
  235.5 60.1 %copy-start.16 = (f32[256]{0:T(256)S(1)}, f32[256]{0:T(256)}, u32[]{:S(2)}) copy-start(f32[256]{0:T(256)} %copy-done.15) | copy-start | bytes 3076
  297.7 1.2 copy-start.7
  298.9 1.2 copy-start.10
  298.9 1.2 copy-start.17
Sparse Core Ops, SparseCore 0:
  12.9 77.3 all-gather.2
  170.5 58.9 all-gather.4
Sparse Core Ops, SparseCore 1:
  96.6 10.9 reduce-scatter.2
  175.8 10.9 reduce-scatter.4
